TPU v7x, 512 devices: a whole 4x8x8 slice. The times are simulated.
512 devices in a mesh: req: 32 (over x, z), tp: 16 (over y, core).
Axes of the slice: x: 4, y: 8, z: 8, core: 2. Of those that a mesh axis runs over, the one named last changes fastest.
Arguments:
- hidden: bfloat16 [32768, 2048], P(('req', 'tp')), may hold values from -6 to 6
- ln_gain: float32 [2048], replicated, may hold values from 0.1 to 1.9
- w_qkv: bfloat16 [2048, 3, 2048], P(None, None, 'tp'), may hold values from -0.125 to 0.125
- w_out: bfloat16 [2048, 2048], P('tp'), may hold values from -0.125 to 0.125
- cache_kv: bfloat16 [2, 512, 256, 2048], P(None, 'req', None, 'tp'), may hold values from -6 to 6
- cache_len: int32 [512], P('req'), may hold values from 16 to 256, as said below
- ancestors: int32 [512, 64, 64], P('req'), may hold values from 0 to 1, as said below
- accepted: int32 [512, 8], P('req'), may hold values from 0 to 14, as said below
Outputs:
- attn_proj: bfloat16 [32768, 2048], P(('req', 'tp'))
- kept_kv: bfloat16 [2, 512, 8, 2048], P(None, 'req', None, 'tp')
Inputs may be any that keep to these rules, and one draw needn't show every extreme that they name: `cache_len`: at least one request of the whole batch has exactly 256 cached positions. `ancestors`: entry (r, i, j) is 1 exactly where draft token j is token i or an ancestor of it in request r's tree; a token's parent has a lower index and token 0 is the root. `accepted`: each row holds, in increasing order, the first 8 tokens of a path down from the root of the request's tree, each entry the parent of the next.
All inputs are finite; a program needn't handle non-finite values.
Results may differ from a plain program's by a relative error of at most 0.018.
Values may be sent and summed in bfloat16 or wider, within the bound.
A program may use at most 64 MiB of HBM per device.

v0:
```python
import math
import jax
import jax.numpy as jnp
from jax import lax
from jax.sharding import PartitionSpec as P

HD = 128
KEY_BLOCK = 128


def block_part(queries, keys, values, positions, valid, slopes):
    heads = queries.shape[2]
    keys_four = keys.reshape(keys.shape[0], keys.shape[1], heads, HD)
    values_four = values.reshape(values.shape[0], values.shape[1], heads, HD)
    scores = jnp.einsum(
        "rihd,rjhd->rhij", queries, keys_four, preferred_element_type=jnp.float32
    ) * (1.0 / math.sqrt(HD))
    scores = scores + slopes[None, :, None, None] * positions[:, None, None, :]
    allowed = valid[:, None, :, :]
    scores = jnp.where(allowed, scores, -1e30)
    top = jnp.max(scores, axis=3)
    expo = jnp.where(allowed, jnp.exp(scores - top[..., None]), 0.0)
    total = jnp.sum(expo, axis=3)
    weights = expo.astype(jnp.bfloat16)
    summed = jnp.einsum("rhij,rjhd->rihd", weights, values_four, preferred_element_type=jnp.float32)
    return (top, total, summed)


def combine(first, second):
    top = jnp.maximum(first[0], second[0])
    scale_one = jnp.exp(first[0] - top)
    scale_two = jnp.exp(second[0] - top)
    total = first[1] * scale_one + second[1] * scale_two
    summed = (
        first[2] * jnp.transpose(scale_one, (0, 2, 1))[..., None]
        + second[2] * jnp.transpose(scale_two, (0, 2, 1))[..., None]
    )
    return (top, total, summed)


def cache_sweep(queries, keys, values, lengths, stride, slopes):
    requests, drafts, heads = (queries.shape[0], queries.shape[1], queries.shape[2])
    start_state = (
        jnp.full((requests, heads, drafts), -1e30, jnp.float32),
        jnp.zeros((requests, heads, drafts), jnp.float32),
        jnp.zeros((requests, drafts, heads, HD), jnp.float32),
    )
    count = keys.shape[1] // KEY_BLOCK

    def advance(block_index, state):
        start = block_index * KEY_BLOCK
        key_block = lax.dynamic_slice_in_dim(keys, start, KEY_BLOCK, 1)
        value_block = lax.dynamic_slice_in_dim(values, start, KEY_BLOCK, 1)
        cells = (start + jnp.arange(KEY_BLOCK)) * stride
        valid = (cells[None, :] < lengths[:, None])[:, None, :]
        positions = jnp.broadcast_to(cells.astype(jnp.float32)[None, :], (requests, KEY_BLOCK))
        return combine(state, block_part(queries, key_block, value_block, positions, valid, slopes))

    return lax.fori_loop(0, count, advance, start_state)


def on_device(hidden, ln_gain, w_qkv, w_out, cache_kv, cache_len, ancestors, accepted):
    values_f = hidden.astype(jnp.float32)
    mean = jnp.mean(values_f, axis=1, keepdims=True)
    centered = values_f - mean
    var = jnp.mean(centered * centered, axis=1, keepdims=True)
    normed = (centered * lax.rsqrt(var + 1e-05) * ln_gain[None, :]).astype(jnp.bfloat16)
    width = w_qkv.shape[2]
    heads = width // HD
    flat_weight = w_qkv.reshape(w_qkv.shape[0], 3 * width)
    joined = jnp.dot(
        lax.all_gather(normed, "tp", axis=0, tiled=True),
        flat_weight,
        preferred_element_type=jnp.float32,
    )
    requests = cache_len.shape[0]
    drafts = ancestors.shape[1]
    joined = joined.astype(jnp.bfloat16).reshape(requests, drafts, 3, heads, HD)
    queries = joined[:, :, 0]
    new_keys = joined[:, :, 1].reshape(requests, drafts, width)
    new_values = joined[:, :, 2].reshape(requests, drafts, width)
    head_ids = lax.axis_index("tp") * heads + jnp.arange(heads)
    all_heads = heads * lax.axis_size("tp")
    slopes = jnp.exp2(-8.0 * (head_ids.astype(jnp.float32) + 1.0) / all_heads)
    depth = jnp.sum(ancestors, axis=2) - 1
    draft_pos = (cache_len[:, None] + depth).astype(jnp.float32)
    draft_part = block_part(queries, new_keys, new_values, draft_pos, ancestors == 1, slopes)
    cache_part = cache_sweep(queries, cache_kv[0], cache_kv[1], cache_len, 1, slopes)
    merged = combine(cache_part, draft_part)
    attn = (merged[2] / jnp.transpose(merged[1], (0, 2, 1))[..., None]).astype(jnp.bfloat16)
    attn = attn.reshape(requests * drafts, width)
    attn_proj = lax.psum_scatter(
        jnp.dot(attn, w_out, preferred_element_type=jnp.float32).astype(jnp.bfloat16),
        "tp",
        scatter_dimension=0,
        tiled=True,
    )
    onehot = (accepted[:, :, None] == jnp.arange(drafts)[None, None, :]).astype(jnp.bfloat16)
    kept_keys = jnp.einsum("rad,rdc->rac", onehot, new_keys, preferred_element_type=jnp.float32)
    kept_values = jnp.einsum("rad,rdc->rac", onehot, new_values, preferred_element_type=jnp.float32)
    kept_kv = jnp.stack([kept_keys, kept_values]).astype(jnp.bfloat16)
    return (attn_proj, kept_kv)


def solution(mesh):
    placed = (
        P(("req", "tp"), None),
        P(),
        P(None, None, "tp"),
        P("tp", None),
        P(None, "req", None, "tp"),
        P("req"),
        P("req", None, None),
        P("req", None),
    )
    return jax.shard_map(
        on_device,
        mesh=mesh,
        in_specs=placed,
        out_specs=(P(("req", "tp"), None), P(None, "req", None, "tp")),
        check_vma=False,
    )
```

profile of v0, /device:TPU:2, one launch (start us, length us, event | category | flops | bytes accessed | tf_op | source)
XLA Modules:
  0.0 154.7 jit_solution(12655179019747754380)
XLA Ops:
  7.2 1.2 convert_reduce_fusion
  8.4 1.2 fusion.33
  9.6 1.8 %fusion.35 = bf16[64,2048]{1,0:T(8,128)(2,1)} fusion(bf16[64,2048]{1,0:T(8,128)(2,1)} %param.10, f32[2048]{0:T(1024)} %param.11, f32[64]{0:T(128)S(1)} %add_rsqrt_fusion, f32[64]{0:T(128)S(1)} %broadcast_multiply_fusion), kind=kLoop, calls=%fused_computation.56 | loop fusion | flops 655360 | bytes 532992 | tf_op jit(solution)/shard_map/convert_element_type | solution.py:67
  11.6 1.2 copy.18
  13.2 2.6 %copy.16 = bf16[2048,3,128]{0,2,1:T(8,128)(2,1)} copy(bf16[2048,3,128]{2,0,1:T(8,128)(2,1)} %param.12) | data formatting | bytes 3145728 | tf_op args[2]
  15.9 0.7 broadcast_compare_fusion.1
  16.7 2.7 %slice_bitcast_fusion = (bf16[16,256,128]{2,1,0:T(8,128)(2,1)S(1)}, bf16[16,256,128]{2,1,0:T(8,128)(2,1)}) fusion(bf16[2,16,256,128]{3,2,1,0:T(8,128)(2,1)} %param.14), kind=kLoop, calls=%fused_computation.48 | loop fusion | bytes 4194304 | tf_op jit(solution)/shard_map/squeeze | solution.py:88
  19.4 41.4 %all-gather.2.cloned.1.call-done = bf16[1024,2048]{1,0:T(8,128)(2,1)} async-done(((bf16[64,2048]{1,0:T(8,128)(2,1)}), bf16[1024,2048]{1,0:T(8,128)(2,1)}) %all-gather.2.cloned.1.call-update) | async-done | bytes 4194320 | tf_op jit(solution)/shard_map/all_gather | solution.py:72
  60.8 5.9 %convolution_convert_fusion.1 = bf16[1024,384]{1,0:T(8,128)(2,1)} fusion(bf16[1024,2048]{1,0:T(8,128)(2,1)} %all-gather.2.cloned.1.call-done, bf16[2048,384]{0,1:T(8,128)(2,1)} %bitcast.129), kind=kOutput, calls=%fused_computation.34 | convolution fusion | flops 1611005952 | bytes 6553600 | tf_op jit(solution)/shard_map/dot_general | solution.py:71
  66.7 2.4 %reshape.195 = bf16[16,64,3,1,128]{4,2,1,0,3:T(4,128)(2,1)S(1)} reshape(bf16[1024,384]{1,0:T(8,128)(2,1)} %convolution_convert_fusion.1) | data formatting | bytes 1572864 | tf_op jit(solution)/shard_map/reshape | solution.py:78
  69.2 2.2 %fusion.53 = (bf16[16,64,1,1,128]{4,2,1,0,3:T(2,128)(2,1)}, bf16[16,64,1,1,128]{4,2,1,0,3:T(2,128)(2,1)}, bf16[16,64,1,1,128]{4,2,1,0,3:T(2,128)(2,1)S(1)}) fusion(bf16[16,64,3,1,128]{4,2,1,0,3:T(4,128)(2,1)S(1)} %reshape.195), kind=kLoop, calls=%fused_computation.86 | loop fusion | bytes 1572864 | tf_op jit(solution)/shard_map/slice | solution.py:81
  71.4 0.8 copy-done.4
  72.2 5.6 %while.18 = (s32[]{:T(128)}, f32[16,1,64]{2,0,1:T(8,128)S(1)}, f32[16,1,64]{2,0,1:T(8,128)S(1)}, f32[16,64,1,128]{3,1,0,2:T(8,128)S(1)}, s32[16]{0:T(128)S(1)}, ...) while((s32[]{:T(128)}, f32[16,1,64]{2,0,1:T(8,128)S(1)}, ...), condition=%wide.region_5.6_spmd.clone, body=%wide.region_2.5_spmd.clone.sunk | while | flops 68954632 | bytes 4032779 | solution.py:59
  72.3 1.6 %fusion.68 = (f32[16,64]{1,0:T(8,128)S(1)}, f32[16,64,128]{2,1,0:T(8,128)S(1)}) fusion(f32[128]{0:T(128)S(1)} %convert_multiply_fusion.3, bf16[16,64,1,128]{3,1,0,2:T(8,128)(2,1)S(1)} %get-tuple-element.324, bf16[16,256,128]{2,1,0:T(8,128)(2,1)} %get-tuple-element.323, s32[]{:T(128)S(6)} %select_n.64, pred[16,128]{1,0:T(8,128)(4,1)S(1)} %broadcast_compare_fusion.3), kind=kOutput, calls=%fused_computation.85.clone.1 | convolution fusion | flops 34077696 | bytes 1317380 | tf_op jit(solution)/shard_map/while/body/eval_jaxpr/rihd,rjhd->rhij/dot_general | solution.py:15
  73.9 0.4 fusion.70
  74.4 0.6 fusion.72
  75.1 1.6 %fusion.68 = (f32[16,64]{1,0:T(8,128)S(1)}, f32[16,64,128]{2,1,0:T(8,128)S(1)}) fusion(f32[128]{0:T(128)S(1)} %convert_multiply_fusion.3, bf16[16,64,1,128]{3,1,0,2:T(8,128)(2,1)S(1)} %get-tuple-element.324, bf16[16,256,128]{2,1,0:T(8,128)(2,1)} %get-tuple-element.323, s32[]{:T(128)S(6)} %select_n.64, pred[16,128]{1,0:T(8,128)(4,1)S(1)} %broadcast_compare_fusion.3), kind=kOutput, calls=%fused_computation.85.clone.1 | convolution fusion | flops 34077696 | bytes 1317380 | tf_op jit(solution)/shard_map/while/body/eval_jaxpr/rihd,rjhd->rhij/dot_general | solution.py:15
  77.1 0.6 fusion.72
  77.8 1.6 %fusion.54 = (f32[16,64]{1,0:T(8,128)S(1)}, f32[16,64,64]{1,2,0:T(8,128)S(1)}) fusion(pred[16,64,64]{1,2,0:T(32,128)(4,1)} %broadcast_compare_fusion.1, f32[16,64]{1,0:T(8,128)S(1)} %convert_multiply_fusion.1, bf16[16,64,1,1,128]{4,2,1,0,3:T(2,128)(2,1)} %get-tuple-element.218, bf16[16,64,1,1,128]{4,2,1,0,3:T(2,128)(2,1)} %copy-done.4), kind=kOutput, calls=%fused_computation.87 | convolution fusion | flops 17038336 | bytes 860160 | tf_op jit(solution)/shard_map/rihd,rjhd->rhij/dot_general | solution.py:15
  79.6 0.6 fusion.28
  80.2 3.2 %convolution_convert_fusion = bf16[1024,2048]{1,0:T(8,128)(2,1)} fusion(bf16[1024,128]{1,0:T(8,128)(2,1)S(1)} %bitcast.130, bf16[128,2048]{1,0:T(8,128)(2,1)S(1)} %copy-done), kind=kOutput, calls=%fused_computation.33 | convolution fusion | flops 538968064 | bytes 4980736 | tf_op jit(solution)/shard_map/dot_general | solution.py:93
  83.4 0.7 copy-done.9
  84.9 0.6 pad_maximum_fusion
  85.6 62.3 %reduce-scatter.2.cloned.1.call-done = bf16[64,2048]{1,0:T(8,128)(2,1)} async-done(((bf16[1024,2048]{1,0:T(8,128)(2,1)}), bf16[64,2048]{1,0:T(8,128)(2,1)}) %reduce-scatter.2.cloned.1.call-update) | async-done | bytes 262160 | tf_op jit(solution)/shard_map/reduce_scatter | solution.py:92
  (48 shorter events, 2.3 us)
Async XLA Ops:
  7.2 73.0 %copy-start = (bf16[128,2048]{1,0:T(8,128)(2,1)S(1)}, bf16[128,2048]{1,0:T(8,128)(2,1)}, u32[]{:S(2)}) copy-start(bf16[128,2048]{1,0:T(8,128)(2,1)} %param.13) | copy-start | bytes 1572868
  7.2 5.6 %copy-start.3 = (s32[16,64,64]{2,1,0:T(8,128)S(1)}, s32[16,64,64]{2,1,0:T(8,128)}, u32[]{:S(2)}) copy-start(s32[16,64,64]{2,1,0:T(8,128)} %param.16) | copy-start | bytes 786436
  7.2 53.6 %all-gather.2.cloned.1.call-start = ((), (), s32[]{:S(2)}) async-start(), calls=%async_computation.1 | async-start | bytes 4456448 | tf_op jit(solution)/shard_map/all_gather | solution.py:72
  11.5 136.4 %reduce-scatter.2.cloned.1.call-start = ((), (), s32[]{:S(2)}) async-start(), calls=%async_computation.2 | async-start | bytes 4456448 | tf_op jit(solution)/shard_map/reduce_scatter | solution.py:92
  12.8 3.1 %copy-start.1 = (s32[16,64,64]{1,2,0:T(8,128)}, s32[16,64,64]{1,2,0:T(8,128)S(1)}, u32[]{:S(2)}) copy-start(s32[16,64,64]{1,2,0:T(8,128)S(1)} %copy.18) | copy-start | bytes 786436
  12.8 3.0 %copy-start.8 = (s32[16]{0:T(128)S(1)}, s32[16]{0:T(128)}, u32[]{:S(2)}) copy-start(s32[16]{0:T(128)} %param.15) | copy-start | bytes 196
  71.4 0.8 copy-start.4
  72.2 7.2 %copy-start.2 = (s32[16,64,64]{1,2,0:T(8,128)S(1)}, s32[16,64,64]{1,2,0:T(8,128)}, u32[]{:S(2)}) copy-start(s32[16,64,64]{1,2,0:T(8,128)} %copy-done.1) | copy-start | bytes 786436
  77.8 1.8 %copy-start.5 = (bf16[16,64,1,1,128]{4,2,1,0,3:T(2,128)(2,1)S(1)}, bf16[16,64,1,1,128]{4,2,1,0,3:T(2,128)(2,1)}, u32[]{:S(2)}) copy-start(bf16[16,64,1,1,128]{4,2,1,0,3:T(2,128)(2,1)} %get-tuple-element.217) | copy-start | bytes 786436
  77.8 1.8 %copy-start.7 = (pred[16,64,64]{1,2,0:T(32,128)(4,1)S(1)}, pred[16,64,64]{1,2,0:T(32,128)(4,1)}, u32[]{:S(2)}) copy-start(pred[16,64,64]{1,2,0:T(32,128)(4,1)} %broadcast_compare_fusion.1) | copy-start | bytes 196612
  83.4 0.7 copy-start.9
  83.4 1.1 copy-start.6
Sparse Core Ops, SparseCore 0:
  11.6 49.1 all-gather.1
  83.5 64.3 reduce-scatter.1
where the time goes:
time: 155 us
  waiting for transfers between devices  104 us (67%)
  matrix products  16.2 us (10%)
  between operations  14.3 us (9%)
  local copies, waits for them, and re-layouts  13.1 us (8%)
  other arithmetic  7.15 us (5%)
    reduce_scatter x1, waiting for transfers between devices, on_device(): lax.psum_scatter(jnp.dot(attn, w_out, preferred_element_type=jnp.float32)...  62.3 us
    all_gather x1, waiting for transfers between devices, on_device(): lax.all_gather(normed, 'tp', axis=0, tiled=True)  41.4 us
    dot_general x1, matrix products, on_device(): jnp.dot(lax.all_gather(normed, 'tp', axis=0, tiled=True), flat_weight, pr...  5.92 us
    unnamed x24, local copies, waits for them, and re-layouts  5.73 us
    dot_general x3, matrix products, block_part(): jnp.einsum('rihd,rjhd->rhij', queries, keys_four, preferred_element_type=...  4.81 us
    dot_general x1, matrix products, on_device(): jnp.dot(attn, w_out, preferred_element_type=jnp.float32)  3.18 us
  transfers between devices with their start and end apart: 2, of which 2 were waited for; matrix products, arithmetic and copies ran while one was open for 6% of the time, Pallas kernels for 0%

commit v1 on v0

--- a/solution.py
+++ b/solution.py
@@ -6,6 +6,13 @@
 
 HD = 128
 KEY_BLOCK = 128
+
+
+def exchange_gather(x, name, dim):
+    devices = lax.axis_size(name)
+    pieces = jnp.stack([x for _ in range(devices)])
+    pieces = lax.all_to_all(pieces, name, split_axis=0, concat_axis=0)
+    return jnp.concatenate(pieces, axis=dim)
 
 
 def block_part(queries, keys, values, positions, valid, slopes):
@@ -69,9 +76,7 @@
     heads = width // HD
     flat_weight = w_qkv.reshape(w_qkv.shape[0], 3 * width)
     joined = jnp.dot(
-        lax.all_gather(normed, "tp", axis=0, tiled=True),
-        flat_weight,
-        preferred_element_type=jnp.float32,
+        exchange_gather(normed, "tp", 0), flat_weight, preferred_element_type=jnp.float32
     )
     requests = cache_len.shape[0]
     drafts = ancestors.shape[1]

time: 155 us -> 213 us (1.37)
  the two profiles are of different devices: /device:TPU:2 before, /device:TPU:27 now
where the time goes in v1:
time: 213 us
  waiting for transfers between devices  153 us (72%)
  matrix products  17.2 us (8%)
  local copies, waits for them, and re-layouts  14.3 us (7%)
  between operations  14.3 us (7%)
  starting transfers between devices  7.82 us (4%)
  other arithmetic  6.42 us (3%)
    all_to_all x1, waiting for transfers between devices, exchange_gather(): pieces = lax.all_to_all(pieces, name, split_axis=0, concat_axis=0)  86.8 us
    reduce_scatter x1, waiting for transfers between devices, on_device(): lax.psum_scatter(jnp.dot(attn, w_out, preferred_element_type=jnp.float32)...  65.8 us
    all_to_all x1, starting transfers between devices, exchange_gather(): pieces = lax.all_to_all(pieces, name, split_axis=0, concat_axis=0)  7.78 us
    dot_general x1, matrix products, on_device(): jnp.dot(exchange_gather(normed, 'tp', 0), flat_weight, preferred_element_...  5.91 us
    dot_general x3, matrix products, block_part(): jnp.einsum('rihd,rjhd->rhij', queries, keys_four, preferred_element_type=...  4.75 us
    unnamed x22, local copies, waits for them, and re-layouts  4.43 us
  transfers between devices with their start and end apart: 2, of which 2 were waited for; matrix products, arithmetic and copies ran while one was open for 4% of the time, Pallas kernels for 0%

profile of v1, /device:TPU:27, one launch (start us, length us, event | category | flops | bytes accessed | tf_op | source)
XLA Modules:
  0.0 212.7 jit_solution(16530677186553712430)
XLA Ops:
  7.2 1.1 convert_reduce_fusion
  8.3 1.2 fusion.33
  9.5 1.1 fusion.35
  10.7 2.5 %stack.11 = bf16[16,64,2048]{2,1,0:T(8,128)(2,1)} broadcast(bf16[64,2048]{1,0:T(8,128)(2,1)S(1)} %fusion.35), dimensions={1,2} | broadcast | bytes 4456448 | tf_op jit(solution)/shard_map/stack | solution.py:13
  13.2 7.8 %all-to-all-start = ((bf16[16,64,2048]{2,1,0:T(8,128)(2,1)}), bf16[16,64,2048]{2,1,0:T(8,128)(2,1)}, u32[]{:S(2)}, u32[]{:S(2)}) async-start(bf16[16,64,2048]{2,1,0:T(8,128)(2,1)} %stack.11), calls=%async_computation | async-start | bytes 8388608 | tf_op jit(solution)/shard_map/all_to_all | solution.py:14
  21.6 2.7 %copy.16 = bf16[2048,3,128]{0,2,1:T(8,128)(2,1)} copy(bf16[2048,3,128]{2,0,1:T(8,128)(2,1)} %param.12) | data formatting | bytes 3145728 | tf_op args[2]
  24.4 0.7 broadcast_compare_fusion.1
  25.1 2.7 %slice_bitcast_fusion = (bf16[16,256,128]{2,1,0:T(8,128)(2,1)S(1)}, bf16[16,256,128]{2,1,0:T(8,128)(2,1)}) fusion(bf16[2,16,256,128]{3,2,1,0:T(8,128)(2,1)} %param.14), kind=kLoop, calls=%fused_computation.48 | loop fusion | bytes 4194304 | tf_op jit(solution)/shard_map/squeeze | solution.py:93
  27.9 86.8 %all-to-all-done = bf16[16,64,2048]{2,1,0:T(8,128)(2,1)} async-done(((bf16[16,64,2048]{2,1,0:T(8,128)(2,1)}), bf16[16,64,2048]{2,1,0:T(8,128)(2,1)}, u32[]{:S(2)}, u32[]{:S(2)}) %all-to-all-start) | async-done | bytes 4194336 | tf_op jit(solution)/shard_map/all_to_all | solution.py:14
  114.7 5.9 %convolution_convert_fusion.1 = bf16[1024,384]{1,0:T(8,128)(2,1)} fusion(bf16[1024,2048]{1,0:T(8,128)(2,1)} %bitcast.1, bf16[2048,384]{0,1:T(8,128)(2,1)} %bitcast.130), kind=kOutput, calls=%fused_computation.34 | convolution fusion | flops 1611005952 | bytes 6553600 | tf_op jit(solution)/shard_map/dot_general | solution.py:78
  120.6 2.4 %reshape.201 = bf16[16,64,3,1,128]{4,2,1,0,3:T(4,128)(2,1)S(1)} reshape(bf16[1024,384]{1,0:T(8,128)(2,1)} %convolution_convert_fusion.1) | data formatting | bytes 1572864 | tf_op jit(solution)/shard_map/reshape | solution.py:83
  123.0 2.2 %fusion.53 = (bf16[16,64,1,1,128]{4,2,1,0,3:T(2,128)(2,1)}, bf16[16,64,1,1,128]{4,2,1,0,3:T(2,128)(2,1)}, bf16[16,64,1,1,128]{4,2,1,0,3:T(2,128)(2,1)S(1)}) fusion(bf16[16,64,3,1,128]{4,2,1,0,3:T(4,128)(2,1)S(1)} %reshape.201), kind=kLoop, calls=%fused_computation.86 | loop fusion | bytes 1572864 | tf_op jit(solution)/shard_map/slice | solution.py:86
  125.2 0.7 copy-done.4
  126.0 5.6 %while.18 = (s32[]{:T(128)}, f32[16,1,64]{2,0,1:T(8,128)S(1)}, f32[16,1,64]{2,0,1:T(8,128)S(1)}, f32[16,64,1,128]{3,1,0,2:T(8,128)S(1)}, s32[16]{0:T(128)S(1)}, ...) while((s32[]{:T(128)}, f32[16,1,64]{2,0,1:T(8,128)S(1)}, ...), condition=%wide.region_5.6_spmd.clone, body=%wide.region_2.5_spmd.clone.sunk | while | flops 68954632 | bytes 4032779 | solution.py:66
  126.1 1.6 fusion.68
  128.2 0.6 fusion.72
  128.9 1.6 fusion.68
  130.9 0.6 fusion.72
  131.6 1.5 fusion.54
  133.3 1.7 fusion.28
  135.0 3.2 %convolution_convert_fusion = bf16[1024,2048]{1,0:T(8,128)(2,1)} fusion(bf16[1024,128]{1,0:T(8,128)(2,1)S(1)} %bitcast.131, bf16[128,2048]{1,0:T(8,128)(2,1)S(1)} %copy-done), kind=kOutput, calls=%fused_computation.33 | convolution fusion | flops 538968064 | bytes 4980736 | tf_op jit(solution)/shard_map/dot_general | solution.py:98
  138.5 0.7 copy-done.5
  139.4 0.6 pad_maximum_fusion
  140.1 65.8 %reduce-scatter.2.cloned.1.call-done = bf16[64,2048]{1,0:T(8,128)(2,1)} async-done(((bf16[1024,2048]{1,0:T(8,128)(2,1)}), bf16[64,2048]{1,0:T(8,128)(2,1)}) %reduce-scatter.2.cloned.1.call-update) | async-done | bytes 262160 | tf_op jit(solution)/shard_map/reduce_scatter | solution.py:97
  (46 shorter events, 2.5 us)
Async XLA Ops:
  7.2 127.8 %copy-start = (bf16[128,2048]{1,0:T(8,128)(2,1)S(1)}, bf16[128,2048]{1,0:T(8,128)(2,1)}, u32[]{:S(2)}) copy-start(bf16[128,2048]{1,0:T(8,128)(2,1)} %param.13) | copy-start | bytes 1572868
  13.2 7.9 %copy-start.3 = (s32[16,64,64]{2,1,0:T(8,128)S(1)}, s32[16,64,64]{2,1,0:T(8,128)}, u32[]{:S(2)}) copy-start(s32[16,64,64]{2,1,0:T(8,128)} %param.16) | copy-start | bytes 786436
  13.2 101.5 %all-to-all-start = ((bf16[16,64,2048]{2,1,0:T(8,128)(2,1)}), bf16[16,64,2048]{2,1,0:T(8,128)(2,1)}, u32[]{:S(2)}, u32[]{:S(2)}) async-start(bf16[16,64,2048]{2,1,0:T(8,128)(2,1)} %stack.11), calls=%async_computation | async-start | bytes 8388608 | tf_op jit(solution)/shard_map/all_to_all | solution.py:14
  20.9 3.4 %copy-start.7 = (s32[16]{0:T(128)S(1)}, s32[16]{0:T(128)}, u32[]{:S(2)}) copy-start(s32[16]{0:T(128)} %param.15) | copy-start | bytes 196
  20.9 184.9 %reduce-scatter.2.cloned.1.call-start = ((), (), s32[]{:S(2)}) async-start(), calls=%async_computation.2 | async-start | bytes 4456448 | tf_op jit(solution)/shard_map/reduce_scatter | solution.py:97
  21.2 3.1 %copy-start.1 = (s32[16,64,64]{1,2,0:T(8,128)}, s32[16,64,64]{1,2,0:T(8,128)S(1)}, u32[]{:S(2)}) copy-start(s32[16,64,64]{1,2,0:T(8,128)S(1)} %copy.18) | copy-start | bytes 786436
  125.2 0.8 copy-start.4
  126.0 7.1 %copy-start.2 = (s32[16,64,64]{1,2,0:T(8,128)S(1)}, s32[16,64,64]{1,2,0:T(8,128)}, u32[]{:S(2)}) copy-start(s32[16,64,64]{1,2,0:T(8,128)} %copy-done.1) | copy-start | bytes 786436
  135.0 3.2 %copy-start.8 = (s32[16,8]{0,1:T(8,128)S(1)}, s32[16,8]{0,1:T(8,128)}, u32[]{:S(2)}) copy-start(s32[16,8]{0,1:T(8,128)} %param.17) | copy-start | bytes 1540
  135.0 3.3 %copy-start.6 = (bf16[16,64,1,1,128]{4,2,1,0,3:T(2,128)(2,1)S(1)}, bf16[16,64,1,1,128]{4,2,1,0,3:T(2,128)(2,1)}, u32[]{:S(2)}) copy-start(bf16[16,64,1,1,128]{4,2,1,0,3:T(2,128)(2,1)} %get-tuple-element.218) | copy-start | bytes 786436
  138.1 1.0 copy-start.5
Sparse Core Ops, SparseCore 0:
  138.3 67.5 reduce-scatter.1
